TPU v7x, 128 devices: a whole 4x4x4 slice. The times are simulated.
128 devices in a mesh: lat: 16 (over x, y), var: 8 (over z, core).
Axes of the slice: x: 4, y: 4, z: 4, core: 2. Of those that a mesh axis runs over, the one named last changes fastest.
Arguments:
- patches: bfloat16 [96, 192, 1024], P('lat', 'var'), may hold values from -6 to 6
- norm_gain: float32 [1024], replicated, may hold values from 0.25 to 1.75
- input_proj: bfloat16 [1024, 3072], replicated, may hold values from -7 to 7
- output_proj: bfloat16 [1024, 1024], replicated, may hold values from -0.1875 to 0.1875
- level_scale: float32 [40, 1024], P('var'), may hold values from 0.1 to 1.9
- level_shift: float32 [40, 1024], P('var'), may hold values from -3 to 3
- head_weight: bfloat16 [40, 1024, 320], P('var', 'lat'), may hold values from -0.1875 to 0.1875
- targets: bfloat16 [40, 96, 192, 320], P('var', 'lat'), may hold values from -6 to 6
- level_counts: int32 [4], replicated, may hold values from 13 to 37
- tile_dataset: int32 [16, 8], P('lat'), may hold values from 0 to 3
- slot_level: int32 [40], P('var'), may hold values from 0 to 39, as said below
Outputs:
- latent: bfloat16 [96, 192, 1024], P('lat', 'var')
- grad_latent: bfloat16 [96, 192, 1024], P('lat', 'var')
- grad_head: float32 [40, 1024, 320], P('var', 'lat')
Inputs may be any that keep to these rules, and one draw needn't show every extreme that they name: `slot_level`: for each j, slots j * 5 to (j + 1) * 5 - 1 hold the levels j * 5 to (j + 1) * 5 - 1 in some order.
All inputs are finite; a program needn't handle non-finite values.
Results may differ from a plain program's by a relative error of at most 0.012.
Values may be sent and summed in bfloat16 or wider, within the bound.
A program may use at most 128 MiB of HBM per device.

v0:
```python
import math
import jax
import jax.numpy as jnp
from jax import lax
from jax.sharding import PartitionSpec as P

HEADS = 16
WH = 6
WW = 12
EPS = 1e-05


def padded(array, sides, width, wrap):
    for axis, dim in sides:
        size, length = (lax.axis_size(axis), array.shape[dim])
        up = [(i, (i + 1) % size) for i in range(size if wrap else size - 1)]
        down = [(j, i) for i, j in up]
        last = lax.slice_in_dim(array, length - width, length, axis=dim)
        initial = lax.slice_in_dim(array, 0, width, axis=dim)
        before = lax.ppermute(last, axis, up)
        after = lax.ppermute(initial, axis, down)
        array = jnp.concatenate([before, array, after], axis=dim)
    return array


def layer_norm(values, gain):
    wide = values.astype(jnp.float32)
    average = jnp.mean(wide, axis=-1, keepdims=True)
    centred = wide - average
    variance = jnp.mean(centred * centred, axis=-1, keepdims=True)
    return (centred * lax.rsqrt(variance + EPS) * gain).astype(jnp.bfloat16)


def window_attention(query_ext, keyval, row_valid, heads):
    ext_rows, ext_cols, width = query_ext.shape
    head_size = width // heads
    win_rows = ext_rows // WH
    win_cols = ext_cols // WW

    def split(values, parts):
        shaped = values.reshape(win_rows, WH, win_cols, WW, parts, heads, head_size)
        return shaped.transpose(0, 2, 1, 3, 4, 5, 6).reshape(
            win_rows * win_cols, WH * WW, parts, heads, head_size
        )

    query_win = split(query_ext, 1)[:, :, 0]
    pairs = split(keyval, 2)
    key_win = pairs[:, :, 0]
    value_win = pairs[:, :, 1]
    key_mask = jnp.broadcast_to(
        row_valid.reshape(win_rows, 1, WH, 1), (win_rows, win_cols, WH, WW)
    ).reshape(win_rows * win_cols, WH * WW)
    scores = jnp.einsum(
        "wqhd,wkhd->whqk", query_win, key_win, preferred_element_type=jnp.float32
    ) / math.sqrt(head_size)
    scores = jnp.where(key_mask[:, None, None, :], scores, -jnp.inf)
    peak = jnp.max(scores, axis=-1, keepdims=True)
    weights = jnp.exp(scores - peak)
    probs = (weights / jnp.sum(weights, axis=-1, keepdims=True)).astype(jnp.bfloat16)
    mixed = jnp.einsum("whqk,wkhd->wqhd", probs, value_win, preferred_element_type=jnp.float32)
    return (
        mixed.reshape(win_rows, win_cols, WH, WW, width)
        .transpose(0, 2, 1, 3, 4)
        .reshape(ext_rows, ext_cols, width)
    )


def slot_terms(piece, target_rows, live_cols, level_scale, level_shift, heads_full):
    piece_wide = piece.astype(jnp.float32)
    rows = (
        piece_wide[None] * level_scale[:, None, None, :] + level_shift[:, None, None, :]
    ).astype(jnp.bfloat16)
    predicted = jnp.einsum("krnd,kdo->krno", rows, heads_full, preferred_element_type=jnp.float32)
    errors = ((predicted - target_rows.astype(jnp.float32)) * live_cols[:, None, :, None]).astype(
        jnp.bfloat16
    )
    back_grad = jnp.einsum("krno,kdo->krnd", errors, heads_full, preferred_element_type=jnp.float32)
    piece_grad = jnp.sum(back_grad * level_scale[:, None, None, :], axis=0)
    head_add = jnp.einsum("krnd,krno->dko", rows, errors, preferred_element_type=jnp.float32)
    return (piece_grad, head_add)


def local(
    patches,
    norm_gain,
    input_proj,
    output_proj,
    level_scale,
    level_shift,
    head_weight,
    targets,
    level_counts,
    tile_dataset,
    slot_level,
):
    band_rows, band_cols, width = patches.shape
    half_rows = WH // 2
    half_cols = WW // 2
    lat_count = lax.axis_size("lat")
    var_count = lax.axis_size("var")
    lat_place = lax.axis_index("lat")
    ext_rows = band_rows + WH
    ext_cols = band_cols + WW
    extended = padded(patches, (("lat", 0),), half_rows, False)
    extended = padded(extended, (("var", 1),), half_cols, True)
    normed_ext = layer_norm(extended, norm_gain)
    keyval = jnp.dot(
        normed_ext.reshape(-1, width), input_proj[:, width:], preferred_element_type=jnp.float32
    )
    keyval = keyval.astype(jnp.bfloat16).reshape(ext_rows, ext_cols, 2 * width)
    normed = normed_ext[half_rows : half_rows + band_rows, half_cols : half_cols + band_cols]
    queries = jnp.dot(
        normed.reshape(-1, width), input_proj[:, :width], preferred_element_type=jnp.float32
    )
    queries = queries.astype(jnp.bfloat16).reshape(band_rows, band_cols, width)
    query_ext = jnp.pad(queries, ((half_rows, WH - half_rows), (half_cols, WW - half_cols), (0, 0)))
    global_row = lat_place * band_rows - half_rows + jnp.arange(ext_rows, dtype=jnp.int32)
    row_valid = (global_row >= 0) & (global_row < lat_count * band_rows)
    mixed = window_attention(query_ext, keyval, row_valid, HEADS)
    attn = mixed[half_rows : half_rows + band_rows, half_cols : half_cols + band_cols].astype(
        jnp.bfloat16
    )
    update = jnp.dot(
        attn.reshape(-1, width), output_proj, preferred_element_type=jnp.float32
    ).reshape(band_rows, band_cols, width)
    latent = (patches.astype(jnp.float32) + update).astype(jnp.bfloat16)
    dataset_row = tile_dataset[0]
    dataset_ids = jnp.arange(level_counts.shape[0], dtype=jnp.int32)
    tile_levels = jnp.sum(
        jnp.where(dataset_row[:, None] == dataset_ids[None, :], level_counts[None, :], 0), axis=1
    )
    live_tiles = (slot_level[None, :] < tile_levels[:, None]).astype(jnp.float32)
    heads_full = lax.all_gather(head_weight, "lat", axis=1, tiled=True)
    tile_ids = jnp.arange(var_count, dtype=jnp.int32)
    piece = lax.all_gather(latent, "var", axis=1, tiled=True)
    piece_cols = piece.shape[1]
    column_tile = jnp.arange(piece_cols, dtype=jnp.int32) // band_cols
    onehot = (column_tile[:, None] == tile_ids[None, :]).astype(jnp.float32)
    column_live = jnp.dot(onehot, live_tiles)
    piece_grad, head_add = slot_terms(
        piece, targets, column_live.T, level_scale, level_shift, heads_full
    )
    latent_terms = piece_grad
    latent_terms, head_terms = (latent_terms, head_add)
    grad_latent = lax.psum_scatter(
        latent_terms.astype(jnp.bfloat16), "var", scatter_dimension=1, tiled=True
    )
    head_terms = head_terms * (1.0 / math.sqrt(lat_count * band_rows * var_count * band_cols))
    share_rows = width // lat_count
    mine = lax.psum_scatter(
        head_terms.astype(jnp.bfloat16), "lat", scatter_dimension=0, tiled=True
    ).astype(jnp.float32)
    grad_head = jnp.transpose(mine, (1, 0, 2))
    return (latent, grad_latent, grad_head)


def solution(mesh):
    in_specs = (
        P("lat", "var", None),
        P(),
        P(),
        P(),
        P("var", None),
        P("var", None),
        P("var", "lat", None),
        P("var", "lat", None, None),
        P(),
        P("lat", None),
        P("var"),
    )
    out_specs = (P("lat", "var", None), P("lat", "var", None), P("var", "lat", None))
    return jax.shard_map(local, mesh=mesh, in_specs=in_specs, out_specs=out_specs, check_vma=False)
```

profile of v0, /device:TPU:0, one launch (start us, length us, event | category | flops | bytes accessed | tf_op | source)
XLA Modules:
  0.0 313.8 jit_solution(12802649083848093492)
XLA Ops:
  8.4 3.6 %collective-permute-start = (bf16[3,24,1024]{2,1,0:T(8,128)(2,1)S(1)}, bf16[3,24,1024]{2,1,0:T(8,128)(2,1)S(1)}, u32[]{:S(2)}, u32[]{:S(2)}) collective-permute-start(bf16[3,24,1024]{2,1,0:T(8,128)(2,1)S(1)} %get-tuple-element.25), channel_id=1, source_target_pairs={{0,8},{8,16},{16,24},{24,32},{32,40},{40,48},{48,56},{56,64},{64,7... | collective-permute-start | bytes 442376 | tf_op jit(solution)/shard_map/ppermute | solution.py:20
  13.3 1.8 collective-permute-done
  16.0 3.1 collective-permute-done.1
  19.3 2.9 collective-permute-start.3
  22.4 3.2 %collective-permute-done.2 = bf16[12,6,1024]{2,1,0:T(8,128)(2,1)S(1)} collective-permute-done((bf16[12,6,1024]{2,1,0:T(8,128)(2,1)S(1)}, bf16[12,6,1024]{2,1,0:T(8,128)(2,1)S(1)}, u32[]{:S(2)}, u32[]{:S(2)}) %collective-permute-start.2) | collective-permute-done | bytes 147488 | tf_op jit(solution)/shard_map/ppermute | solution.py:20
  26.1 1.8 multiply_reduce_fusion.1
  29.7 2.7 reshape.102
  33.7 2.1 fusion.40
  35.9 2.1 reshape.99
  38.0 3.2 %copy.48 = bf16[2,3,6,12,1,16,64]{6,5,3,2,1,0,4:T(8,128)(2,1)} copy(bf16[2,3,6,12,1,16,64]{6,5,3,1,2,0,4:T(8,128)(2,1)} %bitcast.58) | data formatting | bytes 1769472 | tf_op jit(solution)/shard_map/transpose | solution.py:42
  41.2 5.5 %fusion.15 = bf16[432,2048]{1,0:T(8,128)(2,1)} fusion(bf16[1024,3072]{1,0:T(8,128)(2,1)} %param.13, f32[432,1024]{1,0:T(8,128)S(1)} %copy-done.2, f32[1024]{0:T(1024)S(1)} %copy-done.4, f32[432]{0:T(512)S(1)} %rsqrt.13, f32[432]{0:T(512)S(1)} %div.33), kind=kOutput, calls=%fused_computation.22 | convolution fusion | flops 1814593536 | bytes 7740800 | tf_op jit(solution)/shard_map/dot_general | solution.py:107
  46.8 6.4 %reshape_reshape.3 = bf16[2,6,3,12,2,16,64]{6,5,4,3,2,1,0:T(8,128)(2,1)} reshape(bf16[432,2048]{1,0:T(8,128)(2,1)} %fusion.15) | data formatting | bytes 3538944 | tf_op jit(solution)/shard_map/reshape;reshape | solution.py:41
  53.1 2.6 copy.46
  55.7 2.6 fusion.59
  58.3 4.0 %copy.61 = bf16[6,72,1,16,64]{1,4,3,0,2:T(8,128)(2,1)} copy(bf16[6,72,1,16,64]{4,3,2,1,0:T(8,128)(2,1)} %get-tuple-element.18) | data formatting | bytes 1769472
  62.4 4.0 %copy.62 = bf16[6,72,1,16,64]{1,4,3,0,2:T(8,128)(2,1)} copy(bf16[6,72,1,16,64]{4,3,2,1,0:T(8,128)(2,1)} %get-tuple-element.19) | data formatting | bytes 1769472
  66.4 3.1 fusion.25
  69.5 1.8 fusion.62
  71.3 1.9 fusion.34
  73.2 4.0 %copy.52 = bf16[6,72,16,64]{3,2,1,0:T(8,128)(2,1)} copy(bf16[6,72,16,64]{1,3,2,0:T(8,128)(2,1)} %fusion.34) | data formatting | bytes 1769472 | tf_op jit(solution)/shard_map/whqk,wkhd->wqhd/transpose | solution.py:60
  77.2 3.9 %reshape.100 = bf16[2,3,6,12,1024]{4,3,2,1,0:T(8,128)(2,1)} reshape(bf16[6,72,16,64]{3,2,1,0:T(8,128)(2,1)} %copy.52) | data formatting | bytes 1769472 | tf_op jit(solution)/shard_map/reshape | solution.py:62
  83.6 2.3 fusion.43
  87.1 28.5 %all-gather.3.cloned.1.call-done = bf16[6,192,1024]{2,1,0:T(8,128)(2,1)} async-done(((bf16[6,24,1024]{2,1,0:T(8,128)(2,1)}), bf16[6,192,1024]{2,1,0:T(8,128)(2,1)}) %all-gather.3.cloned.1.call-update) | async-done | bytes 2359312 | tf_op jit(solution)/shard_map/all_gather | solution.py:135
  115.6 4.3 %convert_element_type.67 = f32[6,192,1024]{2,1,0:T(8,128)} convert(bf16[6,192,1024]{2,1,0:T(8,128)(2,1)} %all-gather.3.cloned.1.call-done) | non-fusion elementwise | flops 1179648 | bytes 7077888 | tf_op jit(solution)/shard_map/convert_element_type | solution.py:69
  119.9 48.6 %all-gather.5.cloned.1.call-done = bf16[5,1024,320]{2,1,0:T(8,128)(2,1)} async-done(((bf16[5,64,320]{2,1,0:T(8,128)(2,1)}), bf16[5,1024,320]{2,1,0:T(8,128)(2,1)}) %all-gather.5.cloned.1.call-update) | async-done | bytes 3276816 | tf_op jit(solution)/shard_map/all_gather | solution.py:133
  168.5 10.6 %multiply_convert_fusion = bf16[5,6,192,320]{3,2,1,0:T(8,128)(2,1)S(1)} fusion(bf16[5,6,192,320]{3,2,1,0:T(8,128)(2,1)} %param.18, f32[5,192]{1,0:T(8,128)S(1)} %fusion.52, bf16[5,1024,320]{2,1,0:T(8,128)(2,1)} %all-gather.5.cloned.1.call-done, f32[5,1024]{1,0:T(8,128)S(1)} %copy-done.7, f32[5,1024]{1,0:T(8,128)S(1)} %copy-done.6, ...), kind=kOutput, calls=%fused_computation.11 | convolution fusion | flops 3799941120 | bytes 15412992 | tf_op jit(solution)/shard_map/krnd,kdo->krno/dot_general | solution.py:73
  179.2 7.2 %multiply_reduce_fusion = bf16[6,192,1024]{2,1,0:T(8,128)(2,1)S(1)} fusion(f32[5,1024]{1,0:T(8,128)S(1)} %copy-done.6, bf16[5,6,192,320]{3,2,1,0:T(8,128)(2,1)S(1)} %multiply_convert_fusion, bf16[5,1024,320]{2,1,0:T(8,128)(2,1)S(1)} %copy-done.5), kind=kOutput, calls=%fused_computation.1 | convolution fusion | flops 3785490432 | bytes 9342976 | tf_op jit(solution)/shard_map/krno,kdo->krnd/dot_general | solution.py:77
  186.4 1.7 copy.63
  188.2 9.3 %fusion.14 = bf16[1024,5,320]{0,2,1:T(8,128)(2,1)} fusion(bf16[5,6,192,320]{3,2,1,0:T(8,128)(2,1)} %copy-done.11, f32[5,1024]{1,0:T(8,128)S(1)} %copy-done.7, f32[5,1024]{1,0:T(8,128)S(1)} %copy-done.6, f32[6,192,1024]{2,1,0:T(8,128)} %convert_element_type.67), kind=kOutput, calls=%fused_computation.21 | convolution fusion | flops 3795845120 | bytes 11722752 | tf_op jit(solution)/shard_map/krnd,krno->dko/dot_general | solution.py:79
  197.5 8.2 %copy.54 = bf16[1024,5,320]{2,1,0:T(8,128)(2,1)} copy(bf16[1024,5,320]{0,2,1:T(8,128)(2,1)} %fusion.14) | data formatting | bytes 6553600 | tf_op jit(solution)/shard_map/convert_element_type | solution.py:151
  205.7 16.5 %reduce-scatter.7.cloned.1.call-done = bf16[24,6144]{1,0:T(8,128)(2,1)} async-done(((bf16[192,6144]{1,0:T(8,128)(2,1)}), bf16[24,6144]{1,0:T(8,128)(2,1)}) %reduce-scatter.7.cloned.1.call-update) | async-done | bytes 294928
  224.4 80.9 %reduce-scatter.5.cloned.1.call-done = bf16[64,5,320]{2,1,0:T(8,128)(2,1)} async-done(((bf16[1024,5,320]{2,1,0:T(8,128)(2,1)}), bf16[64,5,320]{2,1,0:T(8,128)(2,1)}) %reduce-scatter.5.cloned.1.call-update) | async-done | bytes 204816 | tf_op jit(solution)/shard_map/reduce_scatter | solution.py:150
  (61 shorter events, 15.3 us)
Async XLA Ops:
  7.2 76.4 %copy-start = (bf16[1024,1024]{1,0:T(8,128)(2,1)S(1)}, bf16[1024,1024]{1,0:T(8,128)(2,1)}, u32[]{:S(2)}) copy-start(bf16[1024,1024]{1,0:T(8,128)(2,1)} %param.14) | copy-start | bytes 6291460
  7.2 108.4 %all-gather.3.cloned.1.call-start = ((), (), s32[]{:S(2)}) async-start(), calls=%async_computation.2 | async-start | bytes 2654208 | tf_op jit(solution)/shard_map/all_gather | solution.py:135
  8.4 6.7 %collective-permute-start = (bf16[3,24,1024]{2,1,0:T(8,128)(2,1)S(1)}, bf16[3,24,1024]{2,1,0:T(8,128)(2,1)S(1)}, u32[]{:S(2)}, u32[]{:S(2)}) collective-permute-start(bf16[3,24,1024]{2,1,0:T(8,128)(2,1)S(1)} %get-tuple-element.25), channel_id=1, source_target_pairs={{0,8},{8,16},{16,24},{24,32},{32,40},{40,48},{48,56},{56,64},{64,7... | collective-permute-start | bytes 442376 | tf_op jit(solution)/shard_map/ppermute | solution.py:20
  12.0 7.2 %collective-permute-start.1 = (bf16[3,24,1024]{2,1,0:T(8,128)(2,1)S(1)}, bf16[3,24,1024]{2,1,0:T(8,128)(2,1)S(1)}, u32[]{:S(2)}, u32[]{:S(2)}) collective-permute-start(bf16[3,24,1024]{2,1,0:T(8,128)(2,1)S(1)} %get-tuple-element.24), channel_id=1, source_target_pairs={{8,0},{16,8},{24,16},{32,24},{40,32},{48,40},{56,48},{64,56},{72,6... | collective-permute-start | bytes 442376 | tf_op jit(solution)/shard_map/ppermute | solution.py:21
  19.2 6.3 %collective-permute-start.2 = (bf16[12,6,1024]{2,1,0:T(8,128)(2,1)S(1)}, bf16[12,6,1024]{2,1,0:T(8,128)(2,1)S(1)}, u32[]{:S(2)}, u32[]{:S(2)}) collective-permute-start(bf16[12,6,1024]{2,1,0:T(8,128)(2,1)S(1)} %get-tuple-element.22), channel_id=1, source_target_pairs={{0,1},{1,2},{2,3},{3,4},{4,5},{5,6},{6,7},{7,0},{8,9},{9,10},{10,1... | collective-permute-start | bytes 442376 | tf_op jit(solution)/shard_map/ppermute | solution.py:20
  19.3 6.3 %collective-permute-start.3 = (bf16[12,6,1024]{2,1,0:T(8,128)(2,1)S(1)}, bf16[12,6,1024]{2,1,0:T(8,128)(2,1)S(1)}, u32[]{:S(2)}, u32[]{:S(2)}) collective-permute-start(bf16[12,6,1024]{2,1,0:T(8,128)(2,1)S(1)} %get-tuple-element.23), channel_id=1, source_target_pairs={{1,0},{2,1},{3,2},{4,3},{5,4},{6,5},{7,6},{0,7},{9,8},{10,9},{11,1... | collective-permute-start | bytes 442376 | tf_op jit(solution)/shard_map/ppermute | solution.py:21
  27.9 4.5 %copy-start.4 = (f32[1024]{0:T(1024)S(1)}, f32[1024]{0:T(1024)}, u32[]{:S(2)}) copy-start(f32[1024]{0:T(1024)} %param.12) | copy-start | bytes 12292
  38.0 3.2 %copy-start.2 = (f32[432,1024]{1,0:T(8,128)S(1)}, f32[432,1024]{1,0:T(8,128)}, u32[]{:S(2)}) copy-start(f32[432,1024]{1,0:T(8,128)} %reshape.102) | copy-start | bytes 5308420
  69.5 1.8 copy-start.3
  82.5 4.2 %copy-start.8 = (s32[4]{0:T(128)S(1)}, s32[4]{0:T(128)}, u32[]{:S(2)}) copy-start(s32[4]{0:T(128)} %param.19) | copy-start | bytes 52
  82.5 4.2 %copy-start.9 = (s32[1,8]{1,0:T(1,128)S(1)}, s32[1,8]{1,0:T(1,128)}, u32[]{:S(2)}) copy-start(s32[1,8]{1,0:T(1,128)} %param.20) | copy-start | bytes 100
  82.5 4.3 %copy-start.10 = (s32[5]{0:T(128)S(1)}, s32[5]{0:T(128)}, u32[]{:S(2)}) copy-start(s32[5]{0:T(128)} %param.21) | copy-start | bytes 64
  85.9 82.6 %all-gather.5.cloned.1.call-start = ((), (), s32[]{:S(2)}) async-start(), calls=%async_computation.3 | async-start | bytes 4177920 | tf_op jit(solution)/shard_map/all_gather | solution.py:133
  86.6 135.5 %reduce-scatter.7.cloned.1.call-start = ((), (), s32[]{:S(2)}) async-start(), calls=%async_computation.5 | async-start | bytes 2654208
  87.1 81.5 %copy-start.6 = (f32[5,1024]{1,0:T(8,128)S(1)}, f32[5,1024]{1,0:T(8,128)}, u32[]{:S(2)}) copy-start(f32[5,1024]{1,0:T(8,128)} %param.15) | copy-start | bytes 61444
  87.1 81.5 %copy-start.7 = (f32[5,1024]{1,0:T(8,128)S(1)}, f32[5,1024]{1,0:T(8,128)}, u32[]{:S(2)}) copy-start(f32[5,1024]{1,0:T(8,128)} %param.16) | copy-start | bytes 61444
  168.5 10.6 %copy-start.5 = (bf16[5,1024,320]{2,1,0:T(8,128)(2,1)S(1)}, bf16[5,1024,320]{2,1,0:T(8,128)(2,1)}, u32[]{:S(2)}) copy-start(bf16[5,1024,320]{2,1,0:T(8,128)(2,1)} %all-gather.5.cloned.1.call-done) | copy-start | bytes 9830404
  179.2 7.2 %copy-start.11 = (bf16[5,6,192,320]{3,2,1,0:T(8,128)(2,1)}, bf16[5,6,192,320]{3,2,1,0:T(8,128)(2,1)S(1)}, u32[]{:S(2)}) copy-start(bf16[5,6,192,320]{3,2,1,0:T(8,128)(2,1)S(1)} %multiply_convert_fusion) | copy-start | bytes 11059204
  188.1 117.2 %reduce-scatter.5.cloned.1.call-start = ((), (), s32[]{:S(2)}) async-start(), calls=%async_computation.4 | async-start | bytes 6684672 | tf_op jit(solution)/shard_map/reduce_scatter | solution.py:150
  205.7 101.6 %copy-start.1 = (bf16[1024,1024]{1,0:T(8,128)(2,1)S(1)}, bf16[1024,1024]{1,0:T(8,128)(2,1)}, u32[]{:S(2)}) copy-start(bf16[1024,1024]{1,0:T(8,128)(2,1)} %param.14) | copy-start | bytes 6291460
Sparse Core Ops, SparseCore 0:
  86.0 29.4 all-gather.2
  117.7 50.7 all-gather.4
  188.2 33.9 reduce-scatter.6
  225.5 79.7 reduce-scatter.4
where the time goes:
time: 315 us; the launch traced here: 314 us
  waiting for transfers between devices  183 us (58%)
  local copies, waits for them, and re-layouts  53.8 us (17%)
  matrix products  42.2 us (13%)
  between operations  14 us (4%)
  other arithmetic  12.5 us (4%)
  starting transfers between devices  7.98 us (3%)
    reduce_scatter x1, waiting for transfers between devices, local(): lax.psum_scatter(head_terms.astype(jnp.bfloat16), 'lat', scatter_dimensio...  80.9 us
    all_gather x1, waiting for transfers between devices, local(): heads_full = lax.all_gather(head_weight, 'lat', axis=1, tiled=True)  48.6 us
    all_gather x1, waiting for transfers between devices, local(): piece = lax.all_gather(latent, 'var', axis=1, tiled=True)  28.5 us
    unnamed x5, waiting for transfers between devices  17.3 us
    unnamed x32, local copies, waits for them, and re-layouts  13.9 us
    dot_general x1, matrix products, slot_terms(): jnp.einsum('krnd,kdo->krno', rows, heads_full, preferred_element_type=jnp...  10.6 us
    dot_general x1, matrix products, slot_terms(): jnp.einsum('krnd,krno->dko', rows, errors, preferred_element_type=jnp.flo...  9.29 us
    another operation x2, local copies, waits for them, and re-layouts, split(): shaped = values.reshape(win_rows, WH, win_cols, WW, parts, heads, head_size)  8.98 us
  transfers between devices with their start and end apart: 8, of which 7 were waited for; matrix products, arithmetic and copies ran while one was open for 8% of the time, Pallas kernels for 0%

commit v1 on v0

--- a/solution.py
+++ b/solution.py
@@ -132,7 +132,11 @@
     live_tiles = (slot_level[None, :] < tile_levels[:, None]).astype(jnp.float32)
     heads_full = lax.all_gather(head_weight, "lat", axis=1, tiled=True)
     tile_ids = jnp.arange(var_count, dtype=jnp.int32)
-    piece = lax.all_gather(latent, "var", axis=1, tiled=True)
+    count = lax.axis_size("var")
+    repeats = [count if d == 1 else 1 for d in range(latent.ndim)]
+    piece = lax.all_to_all(
+        jnp.tile(latent, repeats), "var", split_axis=1, concat_axis=1, tiled=True
+    )
     piece_cols = piece.shape[1]
     column_tile = jnp.arange(piece_cols, dtype=jnp.int32) // band_cols
     onehot = (column_tile[:, None] == tile_ids[None, :]).astype(jnp.float32)

time: 315 us -> 284 us (0.902)
  waiting for transfers between devices: 183 us -> 145 us
  starting transfers between devices: 7.98 us -> 14 us
    all_gather x1, waiting for transfers between devices: 48.6 us -> 0.01 us  [local(): heads_full = lax.all_gather(head_weight, 'lat', axis=1, tiled=True)]
    all_to_all x0 -> x1, waiting for transfers between devices: none -> 37.9 us  [local(): lax.all_to_all(jnp.tile(latent, repeats), 'var', split_axis=1, concat_axi...]
    all_gather x1 -> x0, waiting for transfers between devices: 28.5 us -> none  [local(): piece = lax.all_gather(latent, 'var', axis=1, tiled=True)]
    all_to_all x0 -> x1, starting transfers between devices: none -> 5.84 us  [local(): lax.all_to_all(jnp.tile(latent, repeats), 'var', split_axis=1, concat_axi...]
    unnamed x5 -> x4, waiting for transfers between devices: 17.3 us -> 17.3 us
    unnamed x32 -> x34, local copies, waits for them, and re-layouts: 13.9 us -> 13.9 us
  transfers between devices with their start and end apart: 8 -> 8, of which waited for: 7 -> 6; matrix products, arithmetic and copies ran while one was open for 8% -> 31% of each run, Pallas kernels for 0% -> 0%
where the time goes in v1:
time: 284 us; the launch traced here: 283 us
  waiting for transfers between devices  145 us (51%)
  local copies, waits for them, and re-layouts  56 us (20%)
  matrix products  40.9 us (14%)
  starting transfers between devices  14 us (5%)
  between operations  14 us (5%)
  other arithmetic  13.5 us (5%)
    reduce_scatter x1, waiting for transfers between devices, local(): lax.psum_scatter(head_terms.astype(jnp.bfloat16), 'lat', scatter_dimensio...  81.3 us
    all_to_all x1, waiting for transfers between devices, local(): lax.all_to_all(jnp.tile(latent, repeats), 'var', split_axis=1, concat_axi...  37.9 us
    unnamed x4, waiting for transfers between devices  17.3 us
    unnamed x34, local copies, waits for them, and re-layouts  13.9 us
    dot_general x1, matrix products, slot_terms(): jnp.einsum('krnd,kdo->krno', rows, heads_full, preferred_element_type=jnp...  9.92 us
    dot_general x1, matrix products, slot_terms(): jnp.einsum('krnd,krno->dko', rows, errors, preferred_element_type=jnp.flo...  9.29 us
    another operation x2, local copies, waits for them, and re-layouts, split(): shaped = values.reshape(win_rows, WH, win_cols, WW, parts, heads, head_size)  8.98 us
    convert_element_type x1, local copies, waits for them, and re-layouts, local(): head_terms.astype(jnp.bfloat16)  8.18 us
  transfers between devices with their start and end apart: 8, of which 6 were waited for; matrix products, arithmetic and copies ran while one was open for 31% of the time, Pallas kernels for 0%

profile of v1, /device:TPU:0, one launch (start us, length us, event | category | flops | bytes accessed | tf_op | source)
XLA Modules:
  0.0 283.0 jit_solution(8168551677998861052)
XLA Ops:
  8.4 3.6 %collective-permute-start = (bf16[3,24,1024]{2,1,0:T(8,128)(2,1)S(1)}, bf16[3,24,1024]{2,1,0:T(8,128)(2,1)S(1)}, u32[]{:S(2)}, u32[]{:S(2)}) collective-permute-start(bf16[3,24,1024]{2,1,0:T(8,128)(2,1)S(1)} %get-tuple-element.28), channel_id=1, source_target_pairs={{0,8},{8,16},{16,24},{24,32},{32,40},{40,48},{48,56},{56,64},{64,7... | collective-permute-start | bytes 442376 | tf_op jit(solution)/shard_map/ppermute | solution.py:20
  13.3 1.8 collective-permute-done
  16.0 3.1 %collective-permute-done.1 = bf16[3,24,1024]{2,1,0:T(8,128)(2,1)S(1)} collective-permute-done((bf16[3,24,1024]{2,1,0:T(8,128)(2,1)S(1)}, bf16[3,24,1024]{2,1,0:T(8,128)(2,1)S(1)}, u32[]{:S(2)}, u32[]{:S(2)}) %collective-permute-start.1) | collective-permute-done | bytes 147488 | tf_op jit(solution)/shard_map/ppermute | solution.py:21
  19.3 2.9 %collective-permute-start.3 = (bf16[12,6,1024]{2,1,0:T(8,128)(2,1)S(1)}, bf16[12,6,1024]{2,1,0:T(8,128)(2,1)S(1)}, u32[]{:S(2)}, u32[]{:S(2)}) collective-permute-start(bf16[12,6,1024]{2,1,0:T(8,128)(2,1)S(1)} %get-tuple-element.26), channel_id=1, source_target_pairs={{1,0},{2,1},{3,2},{4,3},{5,4},{6,5},{7,6},{0,7},{9,8},{10,9},{11,1... | collective-permute-start | bytes 442376 | tf_op jit(solution)/shard_map/ppermute | solution.py:21
  22.4 3.1 %collective-permute-done.2 = bf16[12,6,1024]{2,1,0:T(8,128)(2,1)S(1)} collective-permute-done((bf16[12,6,1024]{2,1,0:T(8,128)(2,1)S(1)}, bf16[12,6,1024]{2,1,0:T(8,128)(2,1)S(1)}, u32[]{:S(2)}, u32[]{:S(2)}) %collective-permute-start.2) | collective-permute-done | bytes 147488 | tf_op jit(solution)/shard_map/ppermute | solution.py:20
  26.0 1.8 multiply_reduce_fusion.1
  29.7 2.7 reshape.106
  33.7 2.2 fusion.40
  36.0 2.1 reshape.103
  38.1 3.2 %copy.62 = bf16[2,3,6,12,1,16,64]{6,5,3,2,1,0,4:T(8,128)(2,1)} copy(bf16[2,3,6,12,1,16,64]{6,5,3,1,2,0,4:T(8,128)(2,1)} %bitcast.60) | data formatting | bytes 1769472 | tf_op jit(solution)/shard_map/transpose | solution.py:42
  41.3 5.5 %fusion.15 = bf16[432,2048]{1,0:T(8,128)(2,1)} fusion(bf16[1024,3072]{1,0:T(8,128)(2,1)} %param.13, f32[432,1024]{1,0:T(8,128)S(1)} %copy-done.2, f32[1024]{0:T(1024)S(1)} %copy-done.5, f32[432]{0:T(512)S(1)} %rsqrt.13, f32[432]{0:T(512)S(1)} %div.33), kind=kOutput, calls=%fused_computation.22 | convolution fusion | flops 1814593536 | bytes 7740800 | tf_op jit(solution)/shard_map/dot_general | solution.py:107
  46.8 6.4 %reshape_reshape.3 = bf16[2,6,3,12,2,16,64]{6,5,4,3,2,1,0:T(8,128)(2,1)} reshape(bf16[432,2048]{1,0:T(8,128)(2,1)} %fusion.15) | data formatting | bytes 3538944 | tf_op jit(solution)/shard_map/reshape;reshape | solution.py:41
  53.2 2.6 copy.60
  55.8 2.6 fusion.59
  58.4 4.0 %copy.77 = bf16[6,72,1,16,64]{1,4,3,0,2:T(8,128)(2,1)} copy(bf16[6,72,1,16,64]{4,3,2,1,0:T(8,128)(2,1)} %get-tuple-element.21) | data formatting | bytes 1769472
  62.4 4.1 %copy.78 = bf16[6,72,1,16,64]{1,4,3,0,2:T(8,128)(2,1)} copy(bf16[6,72,1,16,64]{4,3,2,1,0:T(8,128)(2,1)} %get-tuple-element.22) | data formatting | bytes 1769472
  66.5 3.1 %fusion.25 = f32[6,16,72,72]{2,3,1,0:T(8,128)S(1)} fusion(bf16[6,72,16,64]{3,2,1,0:T(8,128)(2,1)} %bitcast.61, bf16[6,72,1,16,64]{1,4,3,0,2:T(8,128)(2,1)} %copy.78), kind=kOutput, calls=%fused_computation.30 | convolution fusion | flops 63700992 | bytes 3760128 | tf_op jit(solution)/shard_map/wqhd,wkhd->whqk/dot_general | solution.py:53
  69.6 1.8 fusion.62
  71.5 1.9 fusion.34
  73.3 4.0 %copy.66 = bf16[6,72,16,64]{3,2,1,0:T(8,128)(2,1)} copy(bf16[6,72,16,64]{1,3,2,0:T(8,128)(2,1)} %fusion.34) | data formatting | bytes 1769472 | tf_op jit(solution)/shard_map/whqk,wkhd->wqhd/transpose | solution.py:60
  77.3 3.9 %reshape.104 = bf16[2,3,6,12,1024]{4,3,2,1,0:T(8,128)(2,1)} reshape(bf16[6,72,16,64]{3,2,1,0:T(8,128)(2,1)} %copy.66) | data formatting | bytes 1769472 | tf_op jit(solution)/shard_map/reshape | solution.py:62
  85.5 2.0 tile.4
  87.5 5.8 %all-to-all-start = ((bf16[6,192,1024]{2,0,1:T(8,128)(2,1)}), bf16[6,192,1024]{2,0,1:T(8,128)(2,1)}, u32[]{:S(2)}, u32[]{:S(2)}) async-start(bf16[6,192,1024]{2,0,1:T(8,128)(2,1)} %bitcast.58), calls=%async_computation | async-start | bytes 6291456 | tf_op jit(solution)/shard_map/all_to_all | solution.py:137
  94.0 37.9 %all-to-all-done = bf16[6,192,1024]{2,0,1:T(8,128)(2,1)} async-done(((bf16[6,192,1024]{2,0,1:T(8,128)(2,1)}), bf16[6,192,1024]{2,0,1:T(8,128)(2,1)}, u32[]{:S(2)}, u32[]{:S(2)}) %all-to-all-start) | async-done | bytes 2359328 | tf_op jit(solution)/shard_map/all_to_all | solution.py:137
  131.9 5.4 %copy_convert_fusion = f32[6,192,1024]{2,1,0:T(8,128)} fusion(bf16[6,192,1024]{2,0,1:T(8,128)(2,1)} %all-to-all-done), kind=kLoop, calls=%fused_computation.24 | loop fusion | flops 1179648 | bytes 7077888 | tf_op jit(solution)/shard_map/convert_element_type | solution.py:69
  137.3 9.9 %multiply_convert_fusion = bf16[5,6,192,320]{3,2,1,0:T(8,128)(2,1)S(1)} fusion(bf16[5,6,192,320]{3,2,1,0:T(8,128)(2,1)} %param.18, f32[5,192]{1,0:T(8,128)S(1)} %fusion.52, bf16[5,1024,320]{2,1,0:T(8,128)(2,1)} %all-gather.2.cloned.1.call-done, f32[5,1024]{1,0:T(8,128)S(1)} %copy-done.8, f32[5,1024]{1,0:T(8,128)S(1)} %copy-done.7, ...), kind=kOutput, calls=%fused_computation.11 | convolution fusion | flops 3799941120 | bytes 15412992 | tf_op jit(solution)/shard_map/krnd,kdo->krno/dot_general | solution.py:73
  147.3 7.2 %multiply_reduce_fusion = bf16[6,192,1024]{2,1,0:T(8,128)(2,1)S(1)} fusion(f32[5,1024]{1,0:T(8,128)S(1)} %copy-done.7, bf16[5,6,192,320]{3,2,1,0:T(8,128)(2,1)S(1)} %multiply_convert_fusion, bf16[5,1024,320]{2,1,0:T(8,128)(2,1)S(1)} %copy-done.6), kind=kOutput, calls=%fused_computation.1 | convolution fusion | flops 3785490432 | bytes 9342976 | tf_op jit(solution)/shard_map/krno,kdo->krnd/dot_general | solution.py:77
  154.5 1.7 copy.79
  156.3 9.3 %fusion.14 = bf16[1024,5,320]{0,2,1:T(8,128)(2,1)} fusion(bf16[5,6,192,320]{3,2,1,0:T(8,128)(2,1)} %copy-done.12, f32[5,1024]{1,0:T(8,128)S(1)} %copy-done.8, f32[5,1024]{1,0:T(8,128)S(1)} %copy-done.7, f32[6,192,1024]{2,1,0:T(8,128)} %copy_convert_fusion), kind=kOutput, calls=%fused_computation.21 | convolution fusion | flops 3795845120 | bytes 11722752 | tf_op jit(solution)/shard_map/krnd,krno->dko/dot_general | solution.py:79
  165.6 8.2 %copy.70 = bf16[1024,5,320]{2,1,0:T(8,128)(2,1)} copy(bf16[1024,5,320]{0,2,1:T(8,128)(2,1)} %fusion.14) | data formatting | bytes 6553600 | tf_op jit(solution)/shard_map/convert_element_type | solution.py:155
  173.8 17.3 %reduce-scatter.7.cloned.1.call-done = bf16[24,6144]{1,0:T(8,128)(2,1)} async-done(((bf16[192,6144]{1,0:T(8,128)(2,1)}), bf16[24,6144]{1,0:T(8,128)(2,1)}) %reduce-scatter.7.cloned.1.call-update) | async-done | bytes 294928
  193.2 81.3 %reduce-scatter.5.cloned.1.call-done = bf16[64,5,320]{2,1,0:T(8,128)(2,1)} async-done(((bf16[1024,5,320]{2,1,0:T(8,128)(2,1)}), bf16[64,5,320]{2,1,0:T(8,128)(2,1)}) %reduce-scatter.5.cloned.1.call-update) | async-done | bytes 204816 | tf_op jit(solution)/shard_map/reduce_scatter | solution.py:154
  (64 shorter events, 16.5 us)
Async XLA Ops:
  7.2 76.5 %copy-start = (bf16[1024,1024]{1,0:T(8,128)(2,1)S(1)}, bf16[1024,1024]{1,0:T(8,128)(2,1)}, u32[]{:S(2)}) copy-start(bf16[1024,1024]{1,0:T(8,128)(2,1)} %param.14) | copy-start | bytes 6291460
  7.2 130.1 %all-gather.2.cloned.1.call-start = ((), (), s32[]{:S(2)}) async-start(), calls=%async_computation.3 | async-start | bytes 4177920 | tf_op jit(solution)/shard_map/all_gather | solution.py:133
  8.4 6.7 %collective-permute-start = (bf16[3,24,1024]{2,1,0:T(8,128)(2,1)S(1)}, bf16[3,24,1024]{2,1,0:T(8,128)(2,1)S(1)}, u32[]{:S(2)}, u32[]{:S(2)}) collective-permute-start(bf16[3,24,1024]{2,1,0:T(8,128)(2,1)S(1)} %get-tuple-element.28), channel_id=1, source_target_pairs={{0,8},{8,16},{16,24},{24,32},{32,40},{40,48},{48,56},{56,64},{64,7... | collective-permute-start | bytes 442376 | tf_op jit(solution)/shard_map/ppermute | solution.py:20
  12.0 7.2 %collective-permute-start.1 = (bf16[3,24,1024]{2,1,0:T(8,128)(2,1)S(1)}, bf16[3,24,1024]{2,1,0:T(8,128)(2,1)S(1)}, u32[]{:S(2)}, u32[]{:S(2)}) collective-permute-start(bf16[3,24,1024]{2,1,0:T(8,128)(2,1)S(1)} %get-tuple-element.27), channel_id=1, source_target_pairs={{8,0},{16,8},{24,16},{32,24},{40,32},{48,40},{56,48},{64,56},{72,6... | collective-permute-start | bytes 442376 | tf_op jit(solution)/shard_map/ppermute | solution.py:21
  19.2 6.3 %collective-permute-start.2 = (bf16[12,6,1024]{2,1,0:T(8,128)(2,1)S(1)}, bf16[12,6,1024]{2,1,0:T(8,128)(2,1)S(1)}, u32[]{:S(2)}, u32[]{:S(2)}) collective-permute-start(bf16[12,6,1024]{2,1,0:T(8,128)(2,1)S(1)} %get-tuple-element.25), channel_id=1, source_target_pairs={{0,1},{1,2},{2,3},{3,4},{4,5},{5,6},{6,7},{7,0},{8,9},{9,10},{10,1... | collective-permute-start | bytes 442376 | tf_op jit(solution)/shard_map/ppermute | solution.py:20
  19.3 6.3 %collective-permute-start.3 = (bf16[12,6,1024]{2,1,0:T(8,128)(2,1)S(1)}, bf16[12,6,1024]{2,1,0:T(8,128)(2,1)S(1)}, u32[]{:S(2)}, u32[]{:S(2)}) collective-permute-start(bf16[12,6,1024]{2,1,0:T(8,128)(2,1)S(1)} %get-tuple-element.26), channel_id=1, source_target_pairs={{1,0},{2,1},{3,2},{4,3},{5,4},{6,5},{7,6},{0,7},{9,8},{10,9},{11,1... | collective-permute-start | bytes 442376 | tf_op jit(solution)/shard_map/ppermute | solution.py:21
  27.8 4.5 %copy-start.5 = (f32[1024]{0:T(1024)S(1)}, f32[1024]{0:T(1024)}, u32[]{:S(2)}) copy-start(f32[1024]{0:T(1024)} %param.12) | copy-start | bytes 12292
  38.1 3.3 %copy-start.2 = (f32[432,1024]{1,0:T(8,128)S(1)}, f32[432,1024]{1,0:T(8,128)}, u32[]{:S(2)}) copy-start(f32[432,1024]{1,0:T(8,128)} %reshape.106) | copy-start | bytes 5308420
  69.6 1.8 copy-start.3
  85.3 2.2 copy-start.4
  87.5 6.1 %copy-start.9 = (s32[4]{0:T(128)S(1)}, s32[4]{0:T(128)}, u32[]{:S(2)}) copy-start(s32[4]{0:T(128)} %param.19) | copy-start | bytes 52
  87.5 6.1 %copy-start.10 = (s32[1,8]{1,0:T(1,128)S(1)}, s32[1,8]{1,0:T(1,128)}, u32[]{:S(2)}) copy-start(s32[1,8]{1,0:T(1,128)} %param.20) | copy-start | bytes 100
  87.5 6.2 %copy-start.11 = (s32[5]{0:T(128)S(1)}, s32[5]{0:T(128)}, u32[]{:S(2)}) copy-start(s32[5]{0:T(128)} %param.21) | copy-start | bytes 64
  87.5 44.4 %all-to-all-start = ((bf16[6,192,1024]{2,0,1:T(8,128)(2,1)}), bf16[6,192,1024]{2,0,1:T(8,128)(2,1)}, u32[]{:S(2)}, u32[]{:S(2)}) async-start(bf16[6,192,1024]{2,0,1:T(8,128)(2,1)} %bitcast.58), calls=%async_computation | async-start | bytes 6291456 | tf_op jit(solution)/shard_map/all_to_all | solution.py:137
  93.4 97.6 %reduce-scatter.7.cloned.1.call-start = ((), (), s32[]{:S(2)}) async-start(), calls=%async_computation.5 | async-start | bytes 2654208
  94.0 43.3 %copy-start.7 = (f32[5,1024]{1,0:T(8,128)S(1)}, f32[5,1024]{1,0:T(8,128)}, u32[]{:S(2)}) copy-start(f32[5,1024]{1,0:T(8,128)} %param.15) | copy-start | bytes 61444
  94.0 43.3 %copy-start.8 = (f32[5,1024]{1,0:T(8,128)S(1)}, f32[5,1024]{1,0:T(8,128)}, u32[]{:S(2)}) copy-start(f32[5,1024]{1,0:T(8,128)} %param.16) | copy-start | bytes 61444
  137.3 9.9 %copy-start.6 = (bf16[5,1024,320]{2,1,0:T(8,128)(2,1)S(1)}, bf16[5,1024,320]{2,1,0:T(8,128)(2,1)}, u32[]{:S(2)}) copy-start(bf16[5,1024,320]{2,1,0:T(8,128)(2,1)} %all-gather.2.cloned.1.call-done) | copy-start | bytes 9830404
  147.3 7.2 %copy-start.12 = (bf16[5,6,192,320]{3,2,1,0:T(8,128)(2,1)}, bf16[5,6,192,320]{3,2,1,0:T(8,128)(2,1)S(1)}, u32[]{:S(2)}) copy-start(bf16[5,6,192,320]{3,2,1,0:T(8,128)(2,1)S(1)} %multiply_convert_fusion) | copy-start | bytes 11059204
  156.2 118.3 %reduce-scatter.5.cloned.1.call-start = ((), (), s32[]{:S(2)}) async-start(), calls=%async_computation.4 | async-start | bytes 6684672 | tf_op jit(solution)/shard_map/reduce_scatter | solution.py:154
  173.7 102.7 %copy-start.1 = (bf16[1024,1024]{1,0:T(8,128)(2,1)S(1)}, bf16[1024,1024]{1,0:T(8,128)(2,1)}, u32[]{:S(2)}) copy-start(bf16[1024,1024]{1,0:T(8,128)(2,1)} %param.14) | copy-start | bytes 6291460
Sparse Core Ops, SparseCore 0:
  22.3 52.7 all-gather.1
  156.3 34.6 reduce-scatter.6
  194.5 80.0 reduce-scatter.4
